TPU v7x, 512 devices: a whole 4x4x16 slice. The times are simulated.
512 devices in a mesh: dp: 4 (over x), ep: 128 (over y, z, core).
Axes of the slice: x: 4, y: 4, z: 16, core: 2. Of those that a mesh axis runs over, the one named last changes fastest.
Arguments:
- hidden_states: bfloat16 [4096, 3584], P(('dp', 'ep')), parts along dimension 0, may hold values from -120 to 120
- norm_gain: float32 [3584], replicated, may hold values from 0.1 to 1.9
- expert_ids: int32 [4096, 8], P(('dp', 'ep')), parts along dimension 0, may hold values from 0 to 15, all different within a row; in each aligned block of 8 rows (0 to 7, 8 to 15, ...) at most 5 rows name the same one
- route_scores: float32 [4096, 8], P(('dp', 'ep')), parts along dimension 0, may hold values from 0.1 to 1
- gate_weight: bfloat16 [3584, 16384], P(None, 'ep'), may hold values from -0.09375 to 0.09375
- up_weight: bfloat16 [3584, 16384], P(None, 'ep'), may hold values from -0.09375 to 0.09375
- down_weight: bfloat16 [16384, 3584], P('ep'), may hold values from -0.1875 to 0.1875
- query_latent: bfloat16 [4096, 64, 512], P(('dp', 'ep')), parts along dimension 0, may hold values from -23 to 23
- query_rope: bfloat16 [4096, 4096], P(('dp', 'ep')), parts along dimension 0, may hold values from -23 to 23
- cache_latent: bfloat16 [512, 512, 512], P(('dp', 'ep')), parts along dimension 0, may hold values from -5.3 to 5.3
- cache_rope: bfloat16 [512, 64, 512], P(('dp', 'ep')), parts along dimension 0, may hold values from -5.3 to 5.3
- tree_latent: bfloat16 [4096, 512], P(('dp', 'ep')), parts along dimension 0, may hold values from -6 to 6
- tree_rope: bfloat16 [4096, 64], P(('dp', 'ep')), parts along dimension 0, may hold values from -6 to 6
- cache_lengths: int32 [512], P(('dp', 'ep')), parts along dimension 0, may hold values from 128 to 512, as said below
- tree_parents: int32 [4096], P(('dp', 'ep')), parts along dimension 0, may hold values from 0 to 6, as said below
Outputs:
- attention_out: bfloat16 [4096, 64, 512], P(('dp', 'ep')), parts along dimension 0
- expert_out: bfloat16 [4096, 3584], P(('dp', 'ep')), parts along dimension 0
There are 4 independent parts, one for each index of `dp`. A program takes and returns all parts, laid end to end along the dimension named above; an argument that names none is the same for every part. Nothing has to cross between parts.
Inputs may be any that keep to these rules, and one draw needn't show every extreme that they name: `expert_ids`: in the 8 rows of one device each expert is named by at most 5 rows, a bound that some block reaches; each row names 8 different experts. `cache_lengths`: some request holds exactly 512 positions. `tree_parents`: counting candidates from 0 within their request, candidate i > 0 has a parent below i, and candidate 0 has 0.
All inputs are finite; a program needn't handle non-finite values.
Results may differ from a plain program's by a relative error of at most 0.008.
Values may be sent and summed in bfloat16 or wider, within the bound.
No kernel may reach another device: no remote copies, remote signals or barrier semaphores. Data moves between devices by JAX's collectives and lax.ppermute only.
A program may use at most 64 MiB of HBM per device.

v0:
```python
import jax
import jax.numpy as jnp
from jax import lax
from jax.sharding import PartitionSpec as P

HID = 1024
EXPERTS = 16
MOST = 5


softmax_scale = 192.0 ** (-0.5)
route_scale = 2.5
norm_eps = 1e-06
very_negative = -1e30


def cut_along(value, dim, size):
    before, after = (value.shape[:dim], value.shape[dim + 1 :])
    return jnp.moveaxis(value.reshape(*before, size, -1, *after), dim, 0)


def edges_of(length, count):
    step = length // count
    if step >= 8:
        step -= step % 8
    return [step * k for k in range(1, count)]


def joined_along(blocks, dim):
    dims = list(blocks.shape[1:])
    dims[dim] *= blocks.shape[0]
    return jnp.moveaxis(blocks, 0, dim).reshape(dims)


def exchange_in_pieces(value, axis, pieces, split_dim, concat_dim):
    blocks = cut_along(value, split_dim, lax.axis_size(axis))
    widest = max(range(1, max(2, blocks.ndim - 1)), key=lambda d: blocks.shape[d])
    gathered = []
    for share in jnp.split(blocks, edges_of(blocks.shape[widest], pieces), axis=widest):
        if share.size:
            gathered.append(lax.all_to_all(share, axis, split_axis=0, concat_axis=0, tiled=True))
    return joined_along(jnp.concatenate(gathered, axis=widest), concat_dim)


def side_by_side(arrays, axis, dim, along):
    both = jnp.concatenate(arrays, axis=along)
    out, at, gathered = (lax.all_gather(both, axis, axis=dim, tiled=True), 0, [])
    for a in arrays:
        gathered.append(lax.slice_in_dim(out, at, at + a.shape[along], axis=along))
        at += a.shape[along]
    return tuple(gathered)


def visible_tree(parents):
    tree_size = parents.shape[0]
    position = jnp.arange(tree_size, dtype=jnp.int32)
    parent_map = ((parents[:, None] == position[None, :]) & (position[:, None] > 0)).astype(
        jnp.float32
    )
    identity = jnp.eye(tree_size, dtype=jnp.float32)
    reached = identity
    for sweep_index in range(tree_size):
        reached = jnp.minimum(
            identity + jnp.dot(parent_map, reached, precision=lax.Precision.HIGHEST), 1.0
        )
    return reached > 0.5


def attend_request(
    query_latent,
    query_rope,
    cache_latent,
    cache_rope,
    tree_latent,
    tree_rope,
    cache_length,
    parents,
):
    row_count = query_latent.shape[0]
    head_count = query_latent.shape[1]
    rope_width = tree_rope.shape[1]
    query_rotary = query_rope.reshape(row_count, head_count, rope_width)
    cache_scores = jnp.einsum(
        "rhc,lc->rhl", query_latent, cache_latent, preferred_element_type=jnp.float32
    )
    cache_scores = (
        cache_scores
        + jnp.einsum("rhc,cl->rhl", query_rotary, cache_rope, preferred_element_type=jnp.float32)
    ) * softmax_scale
    candidate_tree_scores = jnp.einsum(
        "rhc,jc->rhj", query_latent, tree_latent, preferred_element_type=jnp.float32
    )
    candidate_tree_scores = (
        candidate_tree_scores
        + jnp.einsum("rhc,jc->rhj", query_rotary, tree_rope, preferred_element_type=jnp.float32)
    ) * softmax_scale
    cache_live = (jnp.arange(cache_latent.shape[0], dtype=jnp.int32) < cache_length)[None, None, :]
    tree_seen = visible_tree(parents)[:, None, :]
    cache_scores = jnp.where(cache_live, cache_scores, very_negative)
    candidate_tree_scores = jnp.where(tree_seen, candidate_tree_scores, very_negative)
    row_peak = jnp.maximum(
        jnp.max(cache_scores, axis=-1, keepdims=True),
        jnp.max(candidate_tree_scores, axis=-1, keepdims=True),
    )
    cache_exp = jnp.where(cache_live, jnp.exp(cache_scores - row_peak), 0.0)
    tree_exp = jnp.where(tree_seen, jnp.exp(candidate_tree_scores - row_peak), 0.0)
    denominator = jnp.sum(cache_exp, axis=-1, keepdims=True) + jnp.sum(
        tree_exp, axis=-1, keepdims=True
    )
    cache_probs = (cache_exp / denominator).astype(jnp.bfloat16)
    tree_probs = (tree_exp / denominator).astype(jnp.bfloat16)
    attended = jnp.einsum(
        "rhl,lc->rhc", cache_probs, cache_latent, preferred_element_type=jnp.float32
    )
    attended = attended + jnp.einsum(
        "rhj,jc->rhc", tree_probs, tree_latent, preferred_element_type=jnp.float32
    )
    return attended.astype(jnp.bfloat16)


def combine_table(expert_ids, route_scores):
    router_weight_matrix = (
        route_scale * route_scores / jnp.sum(route_scores, axis=-1, keepdims=True)
    ).astype(jnp.bfloat16)
    matches = expert_ids[:, :, None] == jnp.arange(EXPERTS, dtype=jnp.int32)[None, None, :]
    return jnp.sum(
        jnp.where(matches, router_weight_matrix.astype(jnp.float32)[:, :, None], 0.0), axis=1
    ).astype(jnp.bfloat16)


def route_plan(merge_expert_outputs, device_ids, unit_count, capacity):
    expert_index = jnp.arange(merge_expert_outputs.shape[1], dtype=jnp.int32)[:, None]
    first_units = device_ids[None, :] * unit_count
    owner = (expert_index * HID < first_units + unit_count) & (
        (expert_index + 1) * HID > first_units
    )
    routed = merge_expert_outputs > 0
    needed = jnp.any(routed[:, :, None] & owner[None, :, :], axis=1)
    needed_count = needed.astype(jnp.int32)
    slot_of = jnp.cumsum(needed_count, axis=0) - needed_count
    placed = needed[:, :, None] & (
        slot_of[:, :, None] == jnp.arange(capacity, dtype=jnp.int32)[None, None, :]
    )
    return jnp.transpose(placed, (1, 2, 0))


def expert_part(arrived_rows, arrived_shares, gate_weight, up_weight, down_weight, first_unit):
    source_count, slot_count, width = arrived_rows.shape
    flat_rows = arrived_rows.reshape(source_count * slot_count, width)
    gate_act = jnp.dot(flat_rows, gate_weight, preferred_element_type=jnp.float32)
    up_act = jnp.dot(flat_rows, up_weight, preferred_element_type=jnp.float32)
    unit_count = gate_weight.shape[1]
    expert_count = arrived_shares.shape[2]
    hidden_unit_expert = (first_unit + jnp.arange(unit_count, dtype=jnp.int32)) // HID
    unit_pick = (
        hidden_unit_expert[None, :] == jnp.arange(expert_count, dtype=jnp.int32)[:, None]
    ).astype(jnp.bfloat16)
    unit_share = jnp.dot(
        arrived_shares.reshape(source_count * slot_count, expert_count),
        unit_pick,
        preferred_element_type=jnp.float32,
    )
    expert_hidden = (unit_share * jax.nn.silu(gate_act) * up_act).astype(jnp.bfloat16)
    partial_out = jnp.dot(expert_hidden, down_weight, preferred_element_type=jnp.float32).reshape(
        source_count, slot_count, width
    )
    return exchange_in_pieces(partial_out.astype(jnp.bfloat16), "ep", 2, 0, 0).astype(
        partial_out.dtype
    )


def local(
    hidden_states,
    norm_gain,
    expert_ids,
    route_scores,
    gate_weight,
    up_weight,
    down_weight,
    query_latent,
    query_rope,
    cache_latent,
    cache_rope,
    tree_latent,
    tree_rope,
    cache_lengths,
    tree_parents,
):
    attention_out = attend_request(
        query_latent,
        query_rope,
        cache_latent[0],
        cache_rope[0],
        tree_latent,
        tree_rope,
        cache_lengths[0],
        tree_parents,
    )
    states = hidden_states.astype(jnp.float32)
    normed = (
        states * lax.rsqrt(jnp.mean(states * states, axis=-1, keepdims=True) + norm_eps) * norm_gain
    ).astype(jnp.bfloat16)
    merge_expert_outputs = combine_table(expert_ids, route_scores)
    device_count = lax.axis_size("ep")
    row_count = normed.shape[0]
    unit_count = gate_weight.shape[1]
    capacity = min(row_count, MOST * max(1, EXPERTS // device_count))
    my_index = lax.axis_index("ep")
    first_unit = my_index * unit_count
    selection = route_plan(
        merge_expert_outputs, jnp.arange(device_count, dtype=jnp.int32), unit_count, capacity
    )
    all_rows, all_shares = side_by_side((normed, merge_expert_outputs), "ep", 0, 1)
    width = all_rows.shape[1]
    expert_count = all_shares.shape[1]
    source_rows = all_rows.reshape(device_count, row_count, width)
    source_shares = all_shares.reshape(device_count, row_count, expert_count)
    mine_only = jnp.reshape(my_index, (1,))
    mine_table = jax.vmap(lambda shares: route_plan(shares, mine_only, unit_count, capacity)[0])(
        source_shares
    ).astype(jnp.bfloat16)
    mine_rows = jnp.einsum(
        "scr,srf->scf", mine_table, source_rows, preferred_element_type=jnp.float32
    ).astype(jnp.bfloat16)
    mine_shares = jnp.einsum(
        "scr,sre->sce", mine_table, source_shares, preferred_element_type=jnp.float32
    ).astype(jnp.bfloat16)
    returned = expert_part(mine_rows, mine_shares, gate_weight, up_weight, down_weight, first_unit)
    expert_out = jnp.einsum(
        "dsr,dsf->rf", selection.astype(jnp.float32), returned, precision=lax.Precision.HIGHEST
    )
    return (attention_out, expert_out.astype(jnp.bfloat16))


def solution(mesh):
    placed = (
        P(("dp", "ep"), None),
        P(),
        P(("dp", "ep"), None),
        P(("dp", "ep"), None),
        P(None, "ep"),
        P(None, "ep"),
        P("ep", None),
        P(("dp", "ep"), None, None),
        P(("dp", "ep"), None),
        P(("dp", "ep"), None, None),
        P(("dp", "ep"), None, None),
        P(("dp", "ep"), None),
        P(("dp", "ep"), None),
        P(("dp", "ep")),
        P(("dp", "ep")),
    )
    return jax.shard_map(
        local,
        mesh=mesh,
        in_specs=placed,
        out_specs=(P(("dp", "ep"), None, None), P(("dp", "ep"), None)),
        check_vma=False,
    )
```

profile of v0, /device:TPU:40, one launch (start us, length us, event | category | flops | bytes accessed | tf_op | source)
XLA Modules:
  0.0 493.0 jit_solution(12676397479905441248)
XLA Ops:
  7.2 0.0 all-gather.2.cloned.1.call-start
  7.2 1.0 fusion.38
  8.3 0.8 reduce_sum.47
  9.1 0.8 fusion.64
  9.8 0.8 select_reduce_fusion
  10.6 0.9 fusion.40
  11.5 0.6 pad_maximum_fusion
  12.2 0.0 all-gather.2.cloned.1.call-update
  12.2 149.0 %all-gather.2.cloned.1.call-done = bf16[1024,3600]{1,0:T(8,128)(2,1)} async-done(((bf16[8,3600]{1,0:T(8,128)(2,1)}), bf16[1024,3600]{1,0:T(8,128)(2,1)}) %all-gather.2.cloned.1.call-update) | async-done | bytes 7372816 | tf_op jit(solution)/shard_map/all_gather | solution.py:47
  161.2 1.2 and_reduce_fusion
  162.4 0.1 and.103
  162.5 0.2 reduce_window_sum.26
  162.7 8.1 %convolution_convert_fusion = bf16[128,5,3584]{2,1,0:T(8,128)(2,1)} fusion(bf16[1024,3600]{1,0:T(8,128)(2,1)} %all-gather.2.cloned.1.call-done, s32[128,8]{1,0:T(8,128)S(1)} %convert_subtract_fusion, pred[128,8]{1,0:T(8,128)(4,1)S(1)} %and.103), kind=kOutput, calls=%fused_computation | convolution fusion | flops 39004160 | bytes 11932672 | tf_op jit(solution)/shard_map/scr,srf->scf/dot_general | solution.py:222
  170.8 8.2 %reshape.255 = bf16[640,3584]{1,0:T(8,128)(2,1)} reshape(bf16[128,5,3584]{2,1,0:T(8,128)(2,1)} %convolution_convert_fusion) | data formatting | bytes 9175040 | tf_op jit(solution)/shard_map/reshape | solution.py:149
  179.1 1.2 convolution_convert_fusion.2
  180.3 0.1 reshape.253
  180.4 3.7 fusion.87
  184.1 0.2 convolution_multiply_fusion.1
  184.3 9.3 %convolution_convert_fusion.1 = bf16[640,3584]{1,0:T(8,128)(2,1)} fusion(bf16[128,3584]{1,0:T(8,128)(2,1)S(1)} %copy-done, f32[640,128]{1,0:T(8,128)S(1)} %convolution_multiply_fusion.1, bf16[640,3584]{1,0:T(8,128)(2,1)} %reshape.255, bf16[3584,128]{1,0:T(8,128)(2,1)S(1)} %copy-done.3), kind=kOutput, calls=%fused_computation.2 | convolution fusion | flops 1176862720 | bytes 11337728 | tf_op jit(solution)/shard_map/dot_general | solution.py:164
  193.7 7.9 %convert_element_type.121 = bf16[128,1,5,3584]{3,2,0,1:T(8,128)(2,1)} reshape(bf16[640,3584]{1,0:T(8,128)(2,1)} %convolution_convert_fusion.1) | data formatting | bytes 9175040 | tf_op jit(solution)/shard_map/convert_element_type | solution.py:167
  201.5 5.6 %slice_bitcast_fusion.3 = bf16[128,1,2,3584]{3,2,1,0:T(2,128)(2,1)} fusion(bf16[128,1,5,3584]{3,2,0,1:T(8,128)(2,1)} %convert_element_type.121), kind=kLoop, calls=%fused_computation.10 | loop fusion | bytes 3670016 | tf_op jit(solution)/shard_map/split | solution.py:39
  207.1 11.2 %all-to-all-start = ((bf16[128,1,2,3584]{3,2,1,0:T(2,128)(2,1)}), bf16[128,1,2,3584]{3,2,1,0:T(2,128)(2,1)S(1)}, u32[]{:S(2)}, u32[]{:S(2)}) async-start(bf16[128,1,2,3584]{3,2,1,0:T(2,128)(2,1)} %slice_bitcast_fusion.3), calls=%async_computation | async-start | bytes 3670016 | tf_op jit(solution)/shard_map/all_to_all | solution.py:41
  218.3 7.0 %slice_bitcast_fusion.2 = bf16[128,1,3,3584]{3,2,1,0:T(4,128)(2,1)} fusion(bf16[128,1,5,3584]{3,2,0,1:T(8,128)(2,1)} %convert_element_type.121), kind=kLoop, calls=%fused_computation.9 | loop fusion | bytes 5505024 | tf_op jit(solution)/shard_map/split | solution.py:39
  225.4 81.5 %all-to-all-done = bf16[128,1,2,3584]{3,2,1,0:T(2,128)(2,1)S(1)} async-done(((bf16[128,1,2,3584]{3,2,1,0:T(2,128)(2,1)}), bf16[128,1,2,3584]{3,2,1,0:T(2,128)(2,1)S(1)}, u32[]{:S(2)}, u32[]{:S(2)}) %all-to-all-start) | async-done | bytes 1835040 | tf_op jit(solution)/shard_map/all_to_all | solution.py:41
  306.9 8.4 %all-to-all-start.1 = ((bf16[128,1,3,3584]{3,2,1,0:T(4,128)(2,1)}), bf16[128,1,3,3584]{3,2,1,0:T(4,128)(2,1)}, u32[]{:S(2)}, u32[]{:S(2)}) async-start(bf16[128,1,3,3584]{3,2,1,0:T(4,128)(2,1)} %slice_bitcast_fusion.2), calls=%async_computation.1 | async-start | bytes 7340032 | tf_op jit(solution)/shard_map/all_to_all | solution.py:41
  316.0 0.1 compare_and_fusion
  316.1 0.1 and_reduce_fusion.1
  316.2 0.2 reshape.251
  316.4 0.9 fusion.18
  317.3 0.8 fusion.17
  318.2 0.8 fusion.16
  319.0 0.8 fusion.15
  319.9 0.8 fusion.14
  320.7 0.8 fusion.13
  321.6 0.8 fusion.12
  322.4 0.9 fusion.19
  323.3 0.3 fusion.52
  323.6 0.9 fusion.86
  324.5 1.5 fusion.23
  326.1 0.4 fusion.85
  326.4 0.1 fusion.42
  326.5 0.3 fusion.20
  326.9 0.5 fusion.21
  327.4 1.2 fusion.7
  328.7 1.4 copy.27
  330.1 152.1 %all-to-all-done.1 = bf16[128,1,3,3584]{3,2,1,0:T(4,128)(2,1)} async-done(((bf16[128,1,3,3584]{3,2,1,0:T(4,128)(2,1)}), bf16[128,1,3,3584]{3,2,1,0:T(4,128)(2,1)}, u32[]{:S(2)}, u32[]{:S(2)}) %all-to-all-start.1) | async-done | bytes 2752544 | tf_op jit(solution)/shard_map/all_to_all | solution.py:41
  482.2 2.6 copy.28
  484.8 1.4 fusion.4
  (33 shorter events, 0.2 us)
Async XLA Ops:
  7.2 177.2 %copy-start = (bf16[128,3584]{1,0:T(8,128)(2,1)S(1)}, bf16[128,3584]{1,0:T(8,128)(2,1)}, u32[]{:S(2)}) copy-start(bf16[128,3584]{1,0:T(8,128)(2,1)} %param.21) | copy-start | bytes 2752516
  7.2 154.0 %all-gather.2.cloned.1.call-start = ((), (), s32[]{:S(2)}) async-start(), calls=%async_computation.2 | async-start | bytes 7661568 | tf_op jit(solution)/shard_map/all_gather | solution.py:47
  170.8 9.6 %copy-start.8 = (bf16[3584,128]{1,0:T(8,128)(2,1)S(1)}, bf16[3584,128]{1,0:T(8,128)(2,1)}, u32[]{:S(2)}) copy-start(bf16[3584,128]{1,0:T(8,128)(2,1)} %param.19) | copy-start | bytes 2752516
  180.3 4.0 copy-start.3
  207.1 99.7 %all-to-all-start = ((bf16[128,1,2,3584]{3,2,1,0:T(2,128)(2,1)}), bf16[128,1,2,3584]{3,2,1,0:T(2,128)(2,1)S(1)}, u32[]{:S(2)}, u32[]{:S(2)}) async-start(bf16[128,1,2,3584]{3,2,1,0:T(2,128)(2,1)} %slice_bitcast_fusion.3), calls=%async_computation | async-start | bytes 3670016 | tf_op jit(solution)/shard_map/all_to_all | solution.py:41
  225.4 90.8 %copy-start.5 = (bf16[8,4096]{1,0:T(8,128)(2,1)S(1)}, bf16[8,4096]{1,0:T(8,128)(2,1)}, u32[]{:S(2)}) copy-start(bf16[8,4096]{1,0:T(8,128)(2,1)} %param.23) | copy-start | bytes 196612
  225.4 97.9 %copy-start.1 = (bf16[8,64,512]{2,1,0:T(8,128)(2,1)S(1)}, bf16[8,64,512]{2,1,0:T(8,128)(2,1)}, u32[]{:S(2)}) copy-start(bf16[8,64,512]{2,1,0:T(8,128)(2,1)} %param.22) | copy-start | bytes 1572868
  225.4 97.9 %copy-start.7 = (bf16[8,512]{1,0:T(8,128)(2,1)S(1)}, bf16[8,512]{1,0:T(8,128)(2,1)}, u32[]{:S(2)}) copy-start(bf16[8,512]{1,0:T(8,128)(2,1)} %param.26) | copy-start | bytes 24580
  225.4 100.7 %copy-start.6 = (bf16[1,64,512]{2,1,0:T(8,128)(2,1)S(1)}, bf16[1,64,512]{2,1,0:T(8,128)(2,1)}, u32[]{:S(2)}) copy-start(bf16[1,64,512]{2,1,0:T(8,128)(2,1)} %param.25) | copy-start | bytes 196612
  306.9 175.3 %all-to-all-start.1 = ((bf16[128,1,3,3584]{3,2,1,0:T(4,128)(2,1)}), bf16[128,1,3,3584]{3,2,1,0:T(4,128)(2,1)}, u32[]{:S(2)}, u32[]{:S(2)}) async-start(bf16[128,1,3,3584]{3,2,1,0:T(4,128)(2,1)} %slice_bitcast_fusion.2), calls=%async_computation.1 | async-start | bytes 7340032 | tf_op jit(solution)/shard_map/all_to_all | solution.py:41
  316.4 10.5 %copy-start.4 = (bf16[1,512,512]{2,1,0:T(8,128)(2,1)S(1)}, bf16[1,512,512]{2,1,0:T(8,128)(2,1)}, u32[]{:S(2)}) copy-start(bf16[1,512,512]{2,1,0:T(8,128)(2,1)} %param.24) | copy-start | bytes 1572868
  330.1 154.7 %copy-start.2 = (bf16[128,1,2,3584]{3,0,2,1:T(8,128)(2,1)S(1)}, bf16[128,1,2,3584]{3,0,2,1:T(8,128)(2,1)}, u32[]{:S(2)}) copy-start(bf16[128,1,2,3584]{3,0,2,1:T(8,128)(2,1)} %copy.27) | copy-start | bytes 5505028
Sparse Core Ops, SparseCore 0:
  12.3 148.8 all-gather.1
where the time goes:
time: 494 us; the launch traced here: 493 us
  waiting for transfers between devices  383 us (78%)
  matrix products  35.7 us (7%)
  local copies, waits for them, and re-layouts  33.2 us (7%)
  starting transfers between devices  19.7 us (4%)
  between operations  15 us (3%)
  other arithmetic  7 us (1%)
    all_to_all x2, waiting for transfers between devices, exchange_in_pieces(): lax.all_to_all(share, axis, split_axis=0, concat_axis=0, tiled=True)  234 us
    all_gather x1, waiting for transfers between devices, side_by_side(): lax.all_gather(both, axis, axis=dim, tiled=True)  149 us
    all_to_all x2, starting transfers between devices, exchange_in_pieces(): lax.all_to_all(share, axis, split_axis=0, concat_axis=0, tiled=True)  19.7 us
    split x2, local copies, waits for them, and re-layouts, exchange_in_pieces(): jnp.split(blocks, edges_of(blocks.shape[widest], pieces), axis=widest)  12.6 us
  transfers between devices with their start and end apart: 3, of which 3 were waited for; matrix products, arithmetic and copies ran while one was open for 4% of the time, Pallas kernels for 0%

commit v1 on v0

v1 whole, which is shorter than its diff:
```python
import jax
import jax.numpy as jnp
from jax import lax
from jax.sharding import Mesh, PartitionSpec as P

HID = 1024
EXPERTS = 16

softmax_scale = 192.0 ** (-0.5)
route_scale = 2.5
norm_eps = 1e-06
very_negative = -1e30
grid_axes = ("dp", "y", "z", "c")


def visible_tree(parents):
    tree_size = parents.shape[0]
    position = jnp.arange(tree_size, dtype=jnp.int32)
    parent_map = ((parents[:, None] == position[None, :]) & (position[:, None] > 0)).astype(
        jnp.float32
    )
    identity = jnp.eye(tree_size, dtype=jnp.float32)
    reached = identity
    for sweep_index in range(tree_size):
        reached = jnp.minimum(
            identity + jnp.dot(parent_map, reached, precision=lax.Precision.HIGHEST), 1.0
        )
    return reached > 0.5


def attend_request(
    query_latent,
    query_rope,
    cache_latent,
    cache_rope,
    tree_latent,
    tree_rope,
    cache_length,
    parents,
):
    row_count = query_latent.shape[0]
    head_count = query_latent.shape[1]
    rope_width = tree_rope.shape[1]
    query_rotary = query_rope.reshape(row_count, head_count, rope_width)
    cache_scores = jnp.einsum(
        "rhc,lc->rhl", query_latent, cache_latent, preferred_element_type=jnp.float32
    )
    cache_scores = (
        cache_scores
        + jnp.einsum("rhc,cl->rhl", query_rotary, cache_rope, preferred_element_type=jnp.float32)
    ) * softmax_scale
    candidate_tree_scores = jnp.einsum(
        "rhc,jc->rhj", query_latent, tree_latent, preferred_element_type=jnp.float32
    )
    candidate_tree_scores = (
        candidate_tree_scores
        + jnp.einsum("rhc,jc->rhj", query_rotary, tree_rope, preferred_element_type=jnp.float32)
    ) * softmax_scale
    cache_live = (jnp.arange(cache_latent.shape[0], dtype=jnp.int32) < cache_length)[None, None, :]
    tree_seen = visible_tree(parents)[:, None, :]
    cache_scores = jnp.where(cache_live, cache_scores, very_negative)
    candidate_tree_scores = jnp.where(tree_seen, candidate_tree_scores, very_negative)
    row_peak = jnp.maximum(
        jnp.max(cache_scores, axis=-1, keepdims=True),
        jnp.max(candidate_tree_scores, axis=-1, keepdims=True),
    )
    cache_exp = jnp.where(cache_live, jnp.exp(cache_scores - row_peak), 0.0)
    tree_exp = jnp.where(tree_seen, jnp.exp(candidate_tree_scores - row_peak), 0.0)
    denominator = jnp.sum(cache_exp, axis=-1, keepdims=True) + jnp.sum(
        tree_exp, axis=-1, keepdims=True
    )
    cache_probs = (cache_exp / denominator).astype(jnp.bfloat16)
    tree_probs = (tree_exp / denominator).astype(jnp.bfloat16)
    attended = jnp.einsum(
        "rhl,lc->rhc", cache_probs, cache_latent, preferred_element_type=jnp.float32
    )
    attended = attended + jnp.einsum(
        "rhj,jc->rhc", tree_probs, tree_latent, preferred_element_type=jnp.float32
    )
    return attended.astype(jnp.bfloat16)


def combine_table(expert_ids, route_scores):
    router_weight_matrix = (
        route_scale * route_scores / jnp.sum(route_scores, axis=-1, keepdims=True)
    ).astype(jnp.bfloat16)
    matches = expert_ids[:, :, None] == jnp.arange(EXPERTS, dtype=jnp.int32)[None, None, :]
    return jnp.sum(
        jnp.where(matches, router_weight_matrix.astype(jnp.float32)[:, :, None], 0.0), axis=1
    ).astype(jnp.bfloat16)


def swap_core(value):
    return lax.ppermute(value, "c", [(0, 1), (1, 0)])


def gated(rows, share, gate_weight, up_weight, down_weight):
    gate_act = jnp.dot(rows, gate_weight, preferred_element_type=jnp.float32)
    up_act = jnp.dot(rows, up_weight, preferred_element_type=jnp.float32)
    hidden = (share * jax.nn.silu(gate_act) * up_act).astype(jnp.bfloat16)
    return jnp.dot(hidden, down_weight, preferred_element_type=jnp.float32)


def local(
    hidden_states,
    norm_gain,
    expert_ids,
    route_scores,
    gate_weight,
    up_weight,
    down_weight,
    query_latent,
    query_rope,
    cache_latent,
    cache_rope,
    tree_latent,
    tree_rope,
    cache_lengths,
    tree_parents,
):
    other = [swap_core(w) for w in (gate_weight, up_weight, down_weight)]
    states = hidden_states.astype(jnp.float32)
    normed = (
        states * lax.rsqrt(jnp.mean(states * states, axis=-1, keepdims=True) + norm_eps) * norm_gain
    ).astype(jnp.bfloat16)
    width = normed.shape[1]
    combine = combine_table(expert_ids, route_scores)
    packed = jnp.concatenate(
        [normed, jnp.pad(combine, ((0, 0), (0, 128 - EXPERTS)))], axis=1
    )
    gathered = lax.all_gather(packed, ("y", "z"), axis=0, tiled=True)

    attention_out = attend_request(
        query_latent,
        query_rope,
        cache_latent[0],
        cache_rope[0],
        tree_latent,
        tree_rope,
        cache_lengths[0],
        tree_parents,
    )

    chip = lax.axis_index("y") * lax.axis_size("z") + lax.axis_index("z")
    unit_count = 2 * gate_weight.shape[1]
    expert = chip * unit_count // HID
    rows = gathered[:, :width]
    shares = gathered[:, width:].astype(jnp.float32)
    share = jnp.sum(
        jnp.where(jnp.arange(shares.shape[1])[None, :] == expert, shares, 0.0),
        axis=1,
        keepdims=True,
    )
    partial = gated(rows, share, gate_weight, up_weight, down_weight) + gated(rows, share, *other)
    expert_out = lax.psum_scatter(
        partial.astype(jnp.bfloat16), ("y", "z"), scatter_dimension=0, tiled=True
    )
    return (attention_out, expert_out)


def solution(mesh):
    devices = mesh.devices.reshape(4, 4, 16, 2)
    grid = Mesh(devices, grid_axes)
    rows = P(grid_axes, None)
    ep = ("y", "z", "c")
    placed = (
        rows,
        P(),
        rows,
        rows,
        P(None, ep),
        P(None, ep),
        P(ep, None),
        P(grid_axes, None, None),
        rows,
        P(grid_axes, None, None),
        P(grid_axes, None, None),
        rows,
        rows,
        P(grid_axes),
        P(grid_axes),
    )
    return jax.shard_map(
        local,
        mesh=grid,
        in_specs=placed,
        out_specs=(P(grid_axes, None, None), rows),
        check_vma=False,
    )
```

time: 494 us -> 897 us (1.82)
  the two profiles are of different devices: /device:TPU:40 before, /device:TPU:2 now
where the time goes in v1:
time: 897 us
  waiting for transfers between devices  838 us (93%)
  matrix products  30.5 us (3%)
  between operations  15 us (2%)
    reduce_scatter x1, waiting for transfers between devices, local(): lax.psum_scatter(partial.astype(jnp.bfloat16), ('y', 'z'), scatter_dimens...  695 us
    all_gather x1, waiting for transfers between devices, local(): gathered = lax.all_gather(packed, ('y', 'z'), axis=0, tiled=True)  144 us
    dot_general x2, matrix products, gated(): return jnp.dot(hidden, down_weight, preferred_element_type=jnp.float32)  19.3 us
  transfers between devices with their start and end apart: 5, of which 2 were waited for; matrix products, arithmetic and copies ran while one was open for 2% of the time, Pallas kernels for 0%

profile of v1, /device:TPU:2, one launch (start us, length us, event | category | flops | bytes accessed | tf_op | source)
XLA Modules:
  0.0 896.7 jit_solution(6409630612788064503)
XLA Ops:
  7.2 0.0 copy-start
  7.2 0.0 all-gather.2.cloned.1.call-start
  7.2 1.0 fusion.54
  8.2 0.8 reduce_sum.57
  9.1 0.8 fusion.76
  9.8 0.9 fusion.56
  10.7 0.8 select_reduce_fusion.1
  11.5 0.6 fusion.58
  12.1 0.0 all-gather.2.cloned.1.call-update
  12.2 0.0 reduce-scatter.2.cloned.1.call-start
  12.2 1.9 collective-permute-start.1
  14.1 2.4 collective-permute-start
  16.6 1.9 collective-permute-start.2
  18.5 143.6 %all-gather.2.cloned.1.call-done = bf16[512,3712]{1,0:T(8,128)(2,1)} async-done(((bf16[8,3712]{1,0:T(8,128)(2,1)}), bf16[512,3712]{1,0:T(8,128)(2,1)}) %all-gather.2.cloned.1.call-update) | async-done | bytes 3801104 | tf_op jit(solution)/shard_map/all_gather | solution.py:131
  162.1 1.2 select_reduce_fusion
  163.2 4.1 fusion.6
  167.4 0.0 collective-permute-done.1
  167.4 0.0 copy-done.1
  167.4 2.4 fusion
  169.8 0.0 copy-done.3
  169.8 0.0 copy-done.4
  169.9 9.0 fusion.18
  178.8 0.0 collective-permute-done
  178.8 0.0 collective-permute-done.2
  178.8 10.4 %add_convert_fusion = bf16[512,3584]{1,0:T(8,128)(2,1)} fusion(f32[512,3584]{1,0:T(8,128)} %fusion.18, bf16[128,3584]{1,0:T(8,128)(2,1)} %collective-permute-done.2, f32[512,128]{1,0:T(8,128)S(1)} %fusion, bf16[3584,128]{1,0:T(8,128)(2,1)S(1)} %collective-permute-done, bf16[512,3712]{1,0:T(8,128)(2,1)} %all-gather.2.cloned.1.call-done, ...), kind=kOutput, calls=%fused_computation | convolution fusion | flops 943652864 | bytes 16779264 | tf_op jit(solution)/shard_map/dot_general | solution.py:101
  189.2 0.0 copy-start.6
  189.2 0.0 reduce-scatter.2.cloned.1.call-update
  189.2 0.0 copy-done.5
  189.2 0.2 reshape.48
  190.1 0.2 fusion.29
  190.3 0.2 fusion.28
  190.5 0.2 fusion.27
  190.7 0.2 fusion.26
  190.9 0.2 fusion.25
  191.1 0.2 fusion.24
  191.3 0.2 fusion.23
  191.5 0.2 fusion.30
  191.7 0.0 copy-done.7
  191.7 0.3 fusion.65
  192.0 0.2 fusion.99
  192.3 0.5 fusion.34
  192.8 0.0 copy-done.6
  192.8 0.4 fusion.98
  193.1 0.1 fusion.59
  193.2 0.3 fusion.31
  193.6 0.5 fusion.32
  194.1 1.2 fusion.10
  195.4 694.5 %reduce-scatter.2.cloned.1.call-done = bf16[8,3584]{1,0:T(8,128)(2,1)} async-done(((bf16[512,3584]{1,0:T(8,128)(2,1)}), bf16[8,3584]{1,0:T(8,128)(2,1)}) %reduce-scatter.2.cloned.1.call-update) | async-done | bytes 57360 | tf_op jit(solution)/shard_map/reduce_scatter | solution.py:155
  (18 shorter events, 0.1 us)
Async XLA Ops:
  7.2 185.1 %copy-start = (bf16[1,512,512]{2,1,0:T(8,128)(2,1)S(1)}, bf16[1,512,512]{2,1,0:T(8,128)(2,1)}, u32[]{:S(2)}) copy-start(bf16[1,512,512]{2,1,0:T(8,128)(2,1)} %param.24) | copy-start | bytes 1572868
  7.2 154.9 %all-gather.2.cloned.1.call-start = ((), (), s32[]{:S(2)}) async-start(), calls=%async_computation.1 | async-start | bytes 3860480 | tf_op jit(solution)/shard_map/all_gather | solution.py:131
  12.2 877.7 %reduce-scatter.2.cloned.1.call-start = ((), (), s32[]{:S(2)}) async-start(), calls=%async_computation.2 | async-start | bytes 3727360 | tf_op jit(solution)/shard_map/reduce_scatter | solution.py:155
  12.2 155.2 %collective-permute-start.1 = (bf16[3584,128]{1,0:T(8,128)(2,1)}, bf16[3584,128]{1,0:T(8,128)(2,1)}, u32[]{:S(2)}, u32[]{:S(2)}) collective-permute-start(bf16[3584,128]{1,0:T(8,128)(2,1)} %param.20), channel_id=1, source_target_pairs={{0,1},{1,0},{2,3},{3,2},{4,5},{5,4},{6,7},{7,6},{8,9},{9,8},{10,11... | collective-permute-start | bytes 2752520 | tf_op jit(solution)/shard_map/ppermute | solution.py:94
  14.1 164.7 %collective-permute-start = (bf16[3584,128]{1,0:T(8,128)(2,1)}, bf16[3584,128]{1,0:T(8,128)(2,1)S(1)}, u32[]{:S(2)}, u32[]{:S(2)}) collective-permute-start(bf16[3584,128]{1,0:T(8,128)(2,1)} %param.19), channel_id=1, source_target_pairs={{0,1},{1,0},{2,3},{3,2},{4,5},{5,4},{6,7},{7,6},{8,9},{9,8},{10,11... | collective-permute-start | bytes 2752520 | tf_op jit(solution)/shard_map/ppermute | solution.py:94
  16.6 162.3 %collective-permute-start.2 = (bf16[128,3584]{1,0:T(8,128)(2,1)}, bf16[128,3584]{1,0:T(8,128)(2,1)}, u32[]{:S(2)}, u32[]{:S(2)}) collective-permute-start(bf16[128,3584]{1,0:T(8,128)(2,1)} %param.21), channel_id=1, source_target_pairs={{0,1},{1,0},{2,3},{3,2},{4,5},{5,4},{6,7},{7,6},{8,9},{9,8},{10,11... | collective-permute-start | bytes 2752520 | tf_op jit(solution)/shard_map/ppermute | solution.py:94
  162.1 5.3 copy-start.1
  167.4 2.4 copy-start.3
  167.4 2.5 copy-start.4
  178.8 10.4 %copy-start.5 = (bf16[8,4096]{1,0:T(8,128)(2,1)S(1)}, bf16[8,4096]{1,0:T(8,128)(2,1)}, u32[]{:S(2)}) copy-start(bf16[8,4096]{1,0:T(8,128)(2,1)} %param.23) | copy-start | bytes 196612
  189.2 1.0 copy-start.9
  189.2 2.5 copy-start.2
  189.2 2.5 copy-start.7
  189.2 2.9 copy-start.8
  189.2 3.6 copy-start.6
Sparse Core Ops, SparseCore 0:
  12.3 149.7 all-gather.1
  189.3 700.4 reduce-scatter.1
